TPU v7x, 128 devices: a whole 4x4x4 slice. The times are simulated.
128 devices in a mesh: grp: 8 (over y_hi, z), gene: 16 (over y_lo, x, core).
Axes of the slice: x: 4, y: 4 (y_hi: 2, y_lo: 2; y = y_hi * 2 + y_lo), z: 4, core: 2. Of those that a mesh axis runs over, the one named last changes fastest.
Arguments:
- counts: int32 [2048, 15360], P('grp', 'gene'), may hold values from 0 to 12
- panels: int32 [15360], P('gene'), may hold values from 0 to 63
- membership: int32 [8, 256], P('grp'), may hold values from 0 to 3, never falling along the last dimension, each value on 1 to 128 neighbouring positions
- w_proj: bfloat16 [15360, 6400], P('gene'), may hold values from -0.0234375 to 0.0234375
- w_qkv_within: bfloat16 [1600, 32, 150], P(None, 'gene'), may hold values from -0.15625 to 0.15625
- w_out_within: bfloat16 [32, 50, 1600], P('gene'), may hold values from -0.4375 to 0.4375
- w_qkv_cross: bfloat16 [1600, 32, 150], P(None, 'gene'), may hold values from -0.15625 to 0.15625
- w_out_cross: bfloat16 [32, 50, 1600], P('gene'), may hold values from -0.4375 to 0.4375
- w_mean: bfloat16 [1600, 15360], P(None, 'gene'), may hold values from -0.25 to 0.25
- w_disp: bfloat16 [1600, 64], replicated, may hold values from -0.25 to 0.25
Outputs:
- cell_loss: float32 [2048], P('grp')
- grad_mean: float32 [1600, 15360], P('grp', 'gene')
- grad_disp: float32 [1600, 64], replicated
Inputs may be any that keep to these rules, and one draw needn't show every extreme that they name: `membership`: group numbers never fall along a row; a group has at most 128 cells.
All inputs are finite; a program needn't handle non-finite values.
Results may differ from a plain program's by a relative error of at most 0.00055.
Values may be sent and summed in bfloat16 or wider, within the bound.
A program may use at most 128 MiB of HBM per device.

v0:
```python
import jax
import jax.numpy as jnp
from jax import lax
from jax.sharding import PartitionSpec as P

EPS = 1e-06
FLOOR = 0.3
TARGET = 10000.0
DISP_BASE = 0.5


def rms_rows(values):
    return values * lax.rsqrt(jnp.mean(values * values, axis=-1, keepdims=True) + EPS)


def head_norm(values):
    return values * lax.rsqrt(jnp.maximum(jnp.mean(values * values, axis=-1, keepdims=True), FLOOR))


def split_heads(qkv, heads):
    qkv = qkv.reshape(qkv.shape[0], heads, 3, -1)
    query = head_norm(qkv[:, :, 0]).astype(jnp.bfloat16)
    keys = head_norm(qkv[:, :, 1]).astype(jnp.bfloat16)
    values = qkv[:, :, 2].astype(jnp.bfloat16)
    return (query, keys, values)


def within_cells(query, keys, values, modules):
    rows, heads, width = query.shape
    cells = rows // modules
    q_all = query.reshape(cells, modules, heads, width)
    k_all = keys.reshape(cells, modules, heads, width)
    v_all = values.reshape(cells, modules, heads, width)
    scores = jnp.einsum(
        "cmhd,cnhd->chmn", q_all, k_all, preferred_element_type=jnp.float32
    ) * width ** (-0.5)
    weights = jnp.exp(scores)
    probs = (weights / jnp.sum(weights, axis=-1, keepdims=True)).astype(jnp.bfloat16)
    mixed = jnp.einsum("chmn,cnhd->cmhd", probs, v_all, preferred_element_type=jnp.float32)
    return mixed.astype(jnp.bfloat16).reshape(rows, heads * width)


def across_cells(query, keys, values, groups, modules):
    rows, heads, width = query.shape
    cells = rows // modules
    q_all = query.reshape(cells, modules, heads, width)
    k_all = keys.reshape(cells, modules, heads, width)
    v_all = values.reshape(cells, modules, heads, width)
    scores = jnp.einsum(
        "cmhd,nmhd->mhcn", q_all, k_all, preferred_element_type=jnp.float32
    ) * width ** (-0.5)
    same = groups[:, None] == groups[None, :]
    weights = jnp.where(same[None, None], jnp.exp(scores), 0.0)
    probs = (weights / jnp.sum(weights, axis=-1, keepdims=True)).astype(jnp.bfloat16)
    mixed = jnp.einsum("mhcn,nmhd->cmhd", probs, v_all, preferred_element_type=jnp.float32)
    return mixed.astype(jnp.bfloat16).reshape(rows, heads * width)


def nb_terms(observed, rate, theta):
    total = theta + rate
    log_total = jnp.log(total)
    nll = -(
        lax.lgamma(observed + theta)
        - lax.lgamma(theta)
        - lax.lgamma(observed + 1.0)
        + theta * (jnp.log(theta) - log_total)
        + observed * (jnp.log(rate) - log_total)
    )
    d_rate = (theta + observed) / total - observed / rate
    d_theta = -(
        lax.digamma(observed + theta)
        - lax.digamma(theta)
        + jnp.log(theta)
        + 1.0
        - log_total
        - (theta + observed) / total
    )
    return (nll, d_rate, d_theta)


def shards(
    counts,
    panels,
    membership,
    w_proj,
    w_qkv_within,
    w_out_within,
    w_qkv_cross,
    w_out_cross,
    w_mean,
    w_disp,
):
    cells, genes_here = counts.shape
    width = w_qkv_within.shape[0]
    heads_here = w_qkv_within.shape[1]
    modules = w_proj.shape[1] // width
    gene_count = lax.axis_size("gene")
    genes_all = genes_here * gene_count
    rows = cells * modules
    share = rows // gene_count
    cell_share = cells // gene_count
    first = lax.axis_index("gene") * share
    observed = counts.astype(jnp.float32)
    library = 1.0 + lax.psum(jnp.sum(observed, axis=1), "gene")
    scaled = jnp.log1p(observed * (TARGET / library)[:, None]).astype(jnp.bfloat16)
    partial_value = jnp.dot(scaled, w_proj, preferred_element_type=jnp.float32).reshape(rows, width)
    tokens = lax.psum(partial_value, "gene")
    normed = rms_rows(tokens).astype(jnp.bfloat16)
    resid = lax.dynamic_slice_in_dim(tokens, first, share, 0)
    flat_within = w_qkv_within.reshape(width, -1)
    query, keys, values = split_heads(
        jnp.dot(normed, flat_within, preferred_element_type=jnp.float32), heads_here
    )
    mixed = within_cells(query, keys, values, modules)
    out_within = w_out_within.reshape(-1, width)
    block = mixed
    resid = resid + lax.psum_scatter(
        jnp.dot(block, out_within, preferred_element_type=jnp.float32),
        "gene",
        scatter_dimension=0,
        tiled=True,
    )
    flat_cross = w_qkv_cross.reshape(width, -1)
    qkv_cross = jnp.dot(
        lax.all_gather(rms_rows(resid).astype(jnp.bfloat16), "gene", axis=0, tiled=True),
        flat_cross,
        preferred_element_type=jnp.float32,
    )
    query, keys, values = split_heads(qkv_cross, heads_here)
    mixed = across_cells(query, keys, values, membership[0], modules)
    out_cross = w_out_cross.reshape(-1, width)
    block = mixed
    resid = resid + lax.psum_scatter(
        jnp.dot(block, out_cross, preferred_element_type=jnp.float32),
        "gene",
        scatter_dimension=0,
        tiled=True,
    )
    pooled = jnp.mean(resid.reshape(cell_share, modules, width), axis=1)
    hidden = lax.all_gather(rms_rows(pooled).astype(jnp.bfloat16), "gene", axis=0, tiled=True)
    panel_count = w_disp.shape[1]
    logit = jnp.dot(hidden, w_mean, preferred_element_type=jnp.float32)
    disp = jnp.dot(hidden, w_disp, preferred_element_type=jnp.float32)
    onehot = (panels[None, :] == jnp.arange(panel_count, dtype=jnp.int32)[:, None]).astype(
        jnp.float32
    )
    theta = jnp.dot(DISP_BASE + jax.nn.softplus(disp), onehot, precision=lax.Precision.HIGHEST)
    rate_scale = (library / genes_all)[:, None]
    rate = rate_scale * jax.nn.softplus(logit)
    nll, d_rate, d_theta = nb_terms(observed, rate, theta)
    norm_scale = (cells * lax.axis_size("grp")) ** (-0.5)
    d_logit = d_rate * rate_scale * jax.nn.sigmoid(logit) * norm_scale
    d_panel = jnp.dot(d_theta, onehot.T, precision=lax.Precision.HIGHEST)
    cell_part = jnp.sum(nll, axis=1)
    hidden_f = hidden.astype(jnp.float32)
    dims = (((0,), (0,)), ((), ()))
    cell_total = lax.psum(cell_part, "gene")
    d_disp = d_panel * jax.nn.sigmoid(disp) * norm_scale
    local_disp = lax.dot_general(hidden_f, d_disp, dims, precision=lax.Precision.HIGHEST)
    grad_disp = lax.psum(local_disp, ("grp", "gene"))
    cell_loss = cell_total / genes_all
    block = hidden_f
    grad_mean = lax.psum_scatter(
        lax.dot_general(block, d_logit, dims, precision=lax.Precision.HIGHEST),
        "grp",
        scatter_dimension=0,
        tiled=True,
    )
    return (cell_loss, grad_mean, grad_disp)


def solution(mesh):
    return jax.shard_map(
        shards,
        mesh=mesh,
        in_specs=(
            P("grp", "gene"),
            P("gene"),
            P("grp", None),
            P("gene", None),
            P(None, "gene", None),
            P("gene", None, None),
            P(None, "gene", None),
            P("gene", None, None),
            P(None, "gene"),
            P(),
        ),
        out_specs=(P("grp"), P("grp", "gene"), P()),
        check_vma=False,
    )
```

profile of v0, /device:TPU:0, one launch (start us, length us, event | category | flops | bytes accessed | tf_op | source)
XLA Modules:
  0.0 771.5 jit_solution(6979199559063120325)
XLA Ops:
  7.2 1.5 convert_reduce_fusion
  8.7 30.4 %psum.28 = f32[256]{0:T(256)S(1)} all-reduce(f32[256]{0:T(256)S(1)} %convert_reduce_fusion), channel_id=1, replica_groups=mesh['grp'=8,'gene'=16] {'gene'}, use_global_device_ids=true, to_apply=%region_1.0 | all-reduce | flops 256 | bytes 2048 | tf_op jit(solution)/shard_map/psum | solution.py:104
  39.2 11.2 %fusion.168 = f32[256,6400]{1,0:T(8,128)} fusion(bf16[960,6400]{1,0:T(8,128)(2,1)} %param.13, s32[256,960]{0,1:T(8,128)} %param.10, f32[256]{0:T(256)S(1)} %get-tuple-element.14), kind=kOutput, calls=%fused_computation.191 | convolution fusion | flops 3146465280 | bytes 19825664 | tf_op jit(solution)/shard_map/dot_general | solution.py:106
  50.4 8.7 %reshape.175 = f32[1024,1600]{1,0:T(8,128)} reshape(f32[256,6400]{1,0:T(8,128)} %fusion.168) | data formatting | bytes 13107200 | tf_op jit(solution)/shard_map/reshape | solution.py:106
  59.2 7.6 copy.115
  67.0 2.3 copy.116
  69.3 2.6 reshape.176
  71.8 2.4 dot_general.55
  75.0 1.9 reshape.178
  76.9 126.4 %all-reduce.3.cloned.1.call-done = f32[1024,1600]{0,1:T(8,128)} async-done(((f32[1024,1600]{0,1:T(8,128)}), f32[1024,1600]{0,1:T(8,128)}) %all-reduce.3.cloned.1.call-update) | async-done | bytes 6553616 | tf_op jit(solution)/shard_map/psum | solution.py:107
  203.3 3.5 multiply_reduce_fusion
  206.8 1.2 copy-done.2
  208.0 2.7 fusion.3
  210.7 1.1 multiply_reduce_fusion.5
  211.9 1.0 rsqrt.70
  212.8 1.0 rsqrt.72
  213.8 2.3 copy.118
  216.1 2.5 copy.119
  218.6 3.9 fusion.165
  222.5 1.5 copy.122
  224.1 1.1 copy.124
  225.3 1.0 copy.117
  226.3 1.9 fusion.7
  228.2 1.3 copy.125
  229.5 1.3 reshape.177
  230.9 4.9 fusion.246
  235.8 72.7 %reduce-scatter.10.cloned.1.call-done = f32[64,1600]{1,0:T(8,128)} async-done(((f32[1024,1600]{1,0:T(8,128)}), f32[64,1600]{1,0:T(8,128)}) %reduce-scatter.10.cloned.1.call-update) | async-done | bytes 409616
  308.5 2.2 copy.147
  310.7 1.7 multiply_reduce_fusion.1
  312.4 0.9 copy-done.4
  313.3 0.8 multiply_convert_fusion.5
  314.1 1.9 copy.128
  316.2 2.3 copy.129
  318.5 2.6 reshape.179
  321.1 2.4 dot_general.61
  324.3 1.8 reshape.181
  326.3 24.3 %all-gather.2.cloned.1.call-done = bf16[1024,1600]{1,0:T(8,128)(2,1)} async-done(((bf16[64,1600]{1,0:T(8,128)(2,1)}), bf16[1024,1600]{1,0:T(8,128)(2,1)}) %all-gather.2.cloned.1.call-update) | async-done | bytes 3276816 | tf_op jit(solution)/shard_map/all_gather | solution.py:125
  350.5 3.7 fusion
  354.3 1.1 multiply_reduce_fusion.3
  356.1 2.4 copy.131
  358.8 2.3 copy.132
  361.1 1.0 rsqrt.77
  362.1 2.0 copy.130
  364.1 1.7 multiply_convert_fusion.2
  365.9 1.8 multiply_convert_fusion.1
  369.0 1.1 copy.137
  370.1 1.3 reshape.180
  371.4 4.9 fusion.247
  376.4 72.3 %reduce-scatter.12.cloned.1.call-done = f32[64,1600]{1,0:T(8,128)} async-done(((f32[1024,1600]{1,0:T(8,128)}), f32[64,1600]{1,0:T(8,128)}) %reduce-scatter.12.cloned.1.call-update) | async-done | bytes 409616
  448.7 2.2 copy.149
  450.9 2.4 add.116
  453.2 2.2 copy.140
  455.4 1.9 reshape.182
  457.3 1.3 reduce_sum.117
  458.8 19.2 %all_gather.7 = bf16[256,1600]{1,0:T(8,128)(2,1)S(1)} all-gather(bf16[16,1600]{1,0:T(8,128)(2,1)S(1)} %multiply_convert_fusion.6), channel_id=1, replica_groups=mesh['grp'=8,'gene'=16] {'gene'}, dimensions={0}, use_global_device_ids=true | all-gather | bytes 870400 | tf_op jit(solution)/shard_map/all_gather | solution.py:140
  478.0 1.1 fusion.249
  479.5 19.0 %add_reduce_fusion = (f32[256]{0:T(256)S(1)}, f32[256,960]{0,1:T(8,128)S(1)}) fusion(s32[256,960]{0,1:T(8,128)S(1)} %copy-done.5, f32[256,960]{0,1:T(8,128)S(1)} %fusion.249, f32[256]{0:T(256)S(1)} %get-tuple-element.13, s32[960]{0:T(1024)S(1)} %copy-done.12, f32[256,64]{0,1:T(8,128)S(1)} %fusion.248), kind=kOutput, calls=%fused_computation.136 | convolution fusion | flops 231927552 | bytes 3020544 | tf_op jit(solution)/shard_map/dot_general | solution.py:147
  498.6 15.5 %fusion.9 = f32[256,64]{0,1:T(8,128)S(1)} fusion(f32[256,960]{0,1:T(8,128)S(1)} %get-tuple-element.18, s32[256,960]{0,1:T(8,128)S(1)} %copy-done.5, f32[256,960]{0,1:T(8,128)S(1)} %fusion.249, f32[256]{0:T(256)S(1)} %get-tuple-element.13, s32[960]{0:T(1024)S(1)} %copy-done.12, f32[256,64]{0,1:T(8,128)S(1)} %fusion.248), kind=kOutput, calls=%fused_computation.26 | convolution fusion | flops 229928960 | bytes 3085056 | tf_op jit(solution)/shard_map/dot_general | solution.py:153
  514.1 1.3 fusion.250
  515.5 8.4 %fusion.107 = f32[1600,960]{1,0:T(8,128)} fusion(bf16[256,1600]{1,0:T(8,128)(2,1)} %copy-done.3, f32[256,960]{0,1:T(8,128)} %copy-done.13, s32[256,960]{0,1:T(8,128)S(1)} %copy-done.6, f32[256,960]{0,1:T(8,128)S(1)} %get-tuple-element.18, f32[256]{0:T(256)S(1)} %get-tuple-element.13), kind=kOutput, calls=%fused_computation.126 | convolution fusion | flops 4723261440 | bytes 9913344 | tf_op jit(solution)/shard_map/dot_general | solution.py:164
  523.9 29.0 %psum.30 = f32[256]{0:T(256)S(1)} all-reduce(f32[256]{0:T(256)S(1)} %neg.22), channel_id=1, replica_groups=mesh['grp'=8,'gene'=16] {'gene'}, use_global_device_ids=true, to_apply=%region_16.17 | all-reduce | flops 256 | bytes 2048 | tf_op jit(solution)/shard_map/psum | solution.py:157
  553.5 106.5 %all-reduce.5.cloned.1.call-done = f32[1600,64]{0,1:T(8,128)} async-done(((f32[1600,64]{0,1:T(8,128)}), f32[1600,64]{0,1:T(8,128)}) %all-reduce.5.cloned.1.call-update) | async-done | bytes 409616 | tf_op jit(solution)/shard_map/psum | solution.py:160
  660.0 102.6 %reduce-scatter.8.cloned.1.call-done = f32[200,960]{1,0:T(8,128)} async-done(((f32[1600,960]{1,0:T(8,128)}), f32[200,960]{1,0:T(8,128)}) %reduce-scatter.8.cloned.1.call-update) | async-done | bytes 768016 | tf_op jit(solution)/shard_map/reduce_scatter | solution.py:163
  762.6 1.8 copy.168
  (60 shorter events, 6.1 us)
Async XLA Ops:
  7.2 470.8 %copy-start = (bf16[1600,960]{0,1:T(8,128)(2,1)S(1)}, bf16[1600,960]{0,1:T(8,128)(2,1)}, u32[]{:S(2)}) copy-start(bf16[1600,960]{0,1:T(8,128)(2,1)} %param.18) | copy-start | bytes 9216004
  7.2 196.1 %all-reduce.3.cloned.1.call-start = ((), (), s32[]{:S(2)}) async-start(), calls=%async_computation.3 | async-start | bytes 13107200 | tf_op jit(solution)/shard_map/psum | solution.py:107
  66.7 7.5 copy-start.8
  66.8 241.7 %reduce-scatter.10.cloned.1.call-start = ((), (), s32[]{:S(2)}) async-start(), calls=%async_computation.7 | async-start | bytes 7241728
  203.3 4.7 copy-start.2
  235.7 114.8 %all-gather.2.cloned.1.call-start = ((), (), s32[]{:S(2)}) async-start(), calls=%async_computation.4 | async-start | bytes 3620864 | tf_op jit(solution)/shard_map/all_gather | solution.py:125
  312.4 0.9 copy-start.4
  315.9 7.6 copy-start.9
  316.0 132.7 %reduce-scatter.12.cloned.1.call-start = ((), (), s32[]{:S(2)}) async-start(), calls=%async_computation.8 | async-start | bytes 7241728
  318.5 7.6 copy-start.11
  365.8 2.5 copy-start.7
  376.3 283.7 %all-reduce.5.cloned.1.call-start = ((), (), s32[]{:S(2)}) async-start(), calls=%async_computation.6 | async-start | bytes 851968 | tf_op jit(solution)/shard_map/psum | solution.py:160
  458.8 20.3 %copy-start.10 = (bf16[1600,64]{0,1:T(8,128)(2,1)S(1)}, bf16[1600,64]{0,1:T(8,128)(2,1)}, u32[]{:S(2)}) copy-start(bf16[1600,64]{0,1:T(8,128)(2,1)} %param.19) | copy-start | bytes 614404
  478.0 36.1 %copy-start.3 = (bf16[256,1600]{1,0:T(8,128)(2,1)}, bf16[256,1600]{1,0:T(8,128)(2,1)S(1)}, u32[]{:S(2)}) copy-start(bf16[256,1600]{1,0:T(8,128)(2,1)S(1)} %all_gather.7) | copy-start | bytes 2457604
  478.0 1.5 copy-start.5
  478.0 1.5 copy-start.12
  479.1 19.4 %copy-start.13 = (f32[256,960]{0,1:T(8,128)}, f32[256,960]{0,1:T(8,128)S(1)}, u32[]{:S(2)}) copy-start(f32[256,960]{0,1:T(8,128)S(1)} %fusion.249) | copy-start | bytes 2949124
  498.6 16.9 %copy-start.6 = (s32[256,960]{0,1:T(8,128)S(1)}, s32[256,960]{0,1:T(8,128)}, u32[]{:S(2)}) copy-start(s32[256,960]{0,1:T(8,128)} %param.10) | copy-start | bytes 2949124
  515.4 247.2 %reduce-scatter.8.cloned.1.call-start = ((), (), s32[]{:S(2)}) async-start(), calls=%async_computation.5 | async-start | bytes 7372800 | tf_op jit(solution)/shard_map/reduce_scatter | solution.py:163
  523.9 240.6 %copy-start.1 = (bf16[1600,960]{0,1:T(8,128)(2,1)S(1)}, bf16[1600,960]{0,1:T(8,128)(2,1)}, u32[]{:S(2)}) copy-start(bf16[1600,960]{0,1:T(8,128)(2,1)} %param.18) | copy-start | bytes 9216004
Sparse Core Ops, SparseCore 0:
  66.9 136.3 all-reduce.2
  235.9 72.5 reduce-scatter.9
  316.1 34.4 all-gather.1
  376.5 72.1 reduce-scatter.11
  515.5 144.4 all-reduce.4
  664.3 98.2 reduce-scatter.7
where the time goes:
time: 777 us; the launch traced here: 772 us
  waiting for transfers between devices  505 us (65%)
  matrix products  80.1 us (10%)
  blocking collectives  78.6 us (10%)
  local copies, waits for them, and re-layouts  74.7 us (10%)
  other arithmetic  17.9 us (2%)
  between operations  14.7 us (2%)
    unnamed x8, waiting for transfers between devices  145 us
    psum x1, waiting for transfers between devices, shards(): tokens = lax.psum(partial_value, 'gene')  126 us
    psum x1, waiting for transfers between devices, shards(): grad_disp = lax.psum(local_disp, ('grp', 'gene'))  107 us
    reduce_scatter x1, waiting for transfers between devices, shards(): lax.psum_scatter(lax.dot_general(block, d_logit, dims, precision=lax.Prec...  103 us
    psum x1, blocking collectives, shards(): library = 1.0 + lax.psum(jnp.sum(observed, axis=1), 'gene')  30.4 us
    psum x1, blocking collectives, shards(): cell_total = lax.psum(cell_part, 'gene')  29 us
    all_gather x1, waiting for transfers between devices, shards(): lax.all_gather(rms_rows(resid).astype(jnp.bfloat16), 'gene', axis=0, tile...  24.3 us
    all_gather x1, blocking collectives, shards(): lax.all_gather(rms_rows(pooled).astype(jnp.bfloat16), 'gene', axis=0, til...  19.2 us
  transfers between devices with their start and end apart: 6, of which 6 were waited for; matrix products, arithmetic and copies ran while one was open for 4% of the time, Pallas kernels for 0%

commit v1 on v0

--- a/solution.py
+++ b/solution.py
@@ -157,7 +157,7 @@
     cell_total = lax.psum(cell_part, "gene")
     d_disp = d_panel * jax.nn.sigmoid(disp) * norm_scale
     local_disp = lax.dot_general(hidden_f, d_disp, dims, precision=lax.Precision.HIGHEST)
-    grad_disp = lax.psum(local_disp, ("grp", "gene"))
+    grad_disp = lax.psum(lax.psum(local_disp, "gene"), "grp")
     cell_loss = cell_total / genes_all
     block = hidden_f
     grad_mean = lax.psum_scatter(

time: 777 us -> 838 us (1.079)
  waiting for transfers between devices: 505 us -> 566 us
    psum x1 -> x2, waiting for transfers between devices: 107 us -> 167 us  [shards(): grad_disp = lax.psum(lax.psum(local_disp, 'gene'), 'grp')]
    unnamed x8 -> x9, waiting for transfers between devices: 145 us -> 145 us
  transfers between devices with their start and end apart: 6 -> 7, of which waited for: 6 -> 7; matrix products, arithmetic and copies ran while one was open for 4% -> 3% of each run, Pallas kernels for 0% -> 0%
where the time goes in v1:
time: 838 us; the launch traced here: 832 us
  waiting for transfers between devices  566 us (68%)
  matrix products  80.1 us (10%)
  blocking collectives  77.8 us (9%)
  local copies, waits for them, and re-layouts  74.7 us (9%)
  other arithmetic  17.9 us (2%)
  between operations  14.7 us (2%)
    psum x2, waiting for transfers between devices, shards(): grad_disp = lax.psum(lax.psum(local_disp, 'gene'), 'grp')  167 us
    unnamed x9, waiting for transfers between devices  145 us
    psum x1, waiting for transfers between devices, shards(): tokens = lax.psum(partial_value, 'gene')  126 us
    reduce_scatter x1, waiting for transfers between devices, shards(): lax.psum_scatter(lax.dot_general(block, d_logit, dims, precision=lax.Prec...  103 us
    psum x1, blocking collectives, shards(): library = 1.0 + lax.psum(jnp.sum(observed, axis=1), 'gene')  30.4 us
    psum x1, blocking collectives, shards(): cell_total = lax.psum(cell_part, 'gene')  28.1 us
    all_gather x1, waiting for transfers between devices, shards(): lax.all_gather(rms_rows(resid).astype(jnp.bfloat16), 'gene', axis=0, tile...  24.3 us
    all_gather x1, blocking collectives, shards(): lax.all_gather(rms_rows(pooled).astype(jnp.bfloat16), 'gene', axis=0, til...  19.2 us
  transfers between devices with their start and end apart: 7, of which 7 were waited for; matrix products, arithmetic and copies ran while one was open for 3% of the time, Pallas kernels for 0%

profile of v1, /device:TPU:0, one launch (start us, length us, event | category | flops | bytes accessed | tf_op | source)
XLA Modules:
  0.0 831.8 jit_solution(10526446550214184352)
XLA Ops:
  7.2 1.5 convert_reduce_fusion
  8.7 30.4 %psum.35 = f32[256]{0:T(256)S(1)} all-reduce(f32[256]{0:T(256)S(1)} %convert_reduce_fusion), channel_id=1, replica_groups=mesh['grp'=8,'gene'=16] {'gene'}, use_global_device_ids=true, to_apply=%region_1.0 | all-reduce | flops 256 | bytes 2048 | tf_op jit(solution)/shard_map/psum | solution.py:104
  39.2 11.2 %fusion.168 = f32[256,6400]{1,0:T(8,128)} fusion(bf16[960,6400]{1,0:T(8,128)(2,1)} %param.13, s32[256,960]{0,1:T(8,128)} %param.10, f32[256]{0:T(256)S(1)} %get-tuple-element.14), kind=kOutput, calls=%fused_computation.191 | convolution fusion | flops 3146465280 | bytes 19825664 | tf_op jit(solution)/shard_map/dot_general | solution.py:106
  50.4 8.7 %reshape.175 = f32[1024,1600]{1,0:T(8,128)} reshape(f32[256,6400]{1,0:T(8,128)} %fusion.168) | data formatting | bytes 13107200 | tf_op jit(solution)/shard_map/reshape | solution.py:106
  59.2 7.6 copy.115
  67.0 2.3 copy.116
  69.3 2.6 reshape.176
  71.8 2.4 dot_general.55
  75.0 1.9 reshape.178
  76.9 126.4 %all-reduce.4.cloned.1.call-done = f32[1024,1600]{0,1:T(8,128)} async-done(((f32[1024,1600]{0,1:T(8,128)}), f32[1024,1600]{0,1:T(8,128)}) %all-reduce.4.cloned.1.call-update) | async-done | bytes 6553616 | tf_op jit(solution)/shard_map/psum | solution.py:107
  203.3 3.5 multiply_reduce_fusion
  206.8 1.2 copy-done.2
  208.0 2.7 fusion.3
  210.7 1.1 multiply_reduce_fusion.5
  211.9 1.0 rsqrt.70
  212.8 1.0 rsqrt.72
  213.8 2.3 copy.118
  216.1 2.5 copy.119
  218.6 3.9 fusion.165
  222.5 1.5 copy.122
  224.1 1.1 copy.124
  225.3 1.0 copy.117
  226.3 1.9 fusion.7
  228.2 1.3 copy.125
  229.5 1.3 reshape.177
  230.9 4.9 fusion.246
  235.8 72.7 %reduce-scatter.10.cloned.1.call-done = f32[64,1600]{1,0:T(8,128)} async-done(((f32[1024,1600]{1,0:T(8,128)}), f32[64,1600]{1,0:T(8,128)}) %reduce-scatter.10.cloned.1.call-update) | async-done | bytes 409616
  308.5 2.2 copy.147
  310.7 1.7 multiply_reduce_fusion.1
  312.4 0.9 copy-done.4
  314.1 1.9 copy.128
  316.2 2.3 copy.129
  318.5 2.6 reshape.179
  321.1 2.4 dot_general.61
  324.3 1.8 reshape.181
  326.3 24.3 %all-gather.2.cloned.1.call-done = bf16[1024,1600]{1,0:T(8,128)(2,1)} async-done(((bf16[64,1600]{1,0:T(8,128)(2,1)}), bf16[1024,1600]{1,0:T(8,128)(2,1)}) %all-gather.2.cloned.1.call-update) | async-done | bytes 3276816 | tf_op jit(solution)/shard_map/all_gather | solution.py:125
  350.5 3.7 fusion
  354.3 1.1 multiply_reduce_fusion.3
  356.1 2.4 copy.131
  358.8 2.3 copy.132
  361.1 1.0 rsqrt.77
  362.1 2.0 copy.130
  364.1 1.7 multiply_convert_fusion.2
  365.9 1.8 multiply_convert_fusion.1
  369.0 1.1 copy.137
  370.1 1.3 reshape.180
  371.4 4.9 fusion.247
  376.4 72.3 %reduce-scatter.12.cloned.1.call-done = f32[64,1600]{1,0:T(8,128)} async-done(((f32[1024,1600]{1,0:T(8,128)}), f32[64,1600]{1,0:T(8,128)}) %reduce-scatter.12.cloned.1.call-update) | async-done | bytes 409616
  448.7 2.2 copy.149
  450.9 2.4 add.118
  453.2 2.2 copy.140
  455.4 1.9 reshape.182
  457.3 1.3 reduce_sum.117
  458.8 19.2 %all_gather.7 = bf16[256,1600]{1,0:T(8,128)(2,1)S(1)} all-gather(bf16[16,1600]{1,0:T(8,128)(2,1)S(1)} %multiply_convert_fusion.6), channel_id=1, replica_groups=mesh['grp'=8,'gene'=16] {'gene'}, dimensions={0}, use_global_device_ids=true | all-gather | bytes 870400 | tf_op jit(solution)/shard_map/all_gather | solution.py:140
  478.0 1.1 fusion.249
  479.5 19.0 %add_reduce_fusion = (f32[256]{0:T(256)S(1)}, f32[256,960]{0,1:T(8,128)S(1)}) fusion(s32[256,960]{0,1:T(8,128)S(1)} %copy-done.5, f32[256,960]{0,1:T(8,128)S(1)} %fusion.249, f32[256]{0:T(256)S(1)} %get-tuple-element.13, s32[960]{0:T(1024)S(1)} %copy-done.12, f32[256,64]{0,1:T(8,128)S(1)} %fusion.248), kind=kOutput, calls=%fused_computation.136 | convolution fusion | flops 231927552 | bytes 3020544 | tf_op jit(solution)/shard_map/dot_general | solution.py:147
  498.6 15.5 %fusion.9 = f32[256,64]{0,1:T(8,128)S(1)} fusion(f32[256,960]{0,1:T(8,128)S(1)} %get-tuple-element.18, s32[256,960]{0,1:T(8,128)S(1)} %copy-done.5, f32[256,960]{0,1:T(8,128)S(1)} %fusion.249, f32[256]{0:T(256)S(1)} %get-tuple-element.13, s32[960]{0:T(1024)S(1)} %copy-done.12, f32[256,64]{0,1:T(8,128)S(1)} %fusion.248), kind=kOutput, calls=%fused_computation.26 | convolution fusion | flops 229928960 | bytes 3085056 | tf_op jit(solution)/shard_map/dot_general | solution.py:153
  514.1 1.3 fusion.250
  515.5 114.7 %all-reduce.6.cloned.1.call-done = f32[1600,64]{0,1:T(8,128)} async-done(((f32[1600,64]{0,1:T(8,128)}), f32[1600,64]{0,1:T(8,128)}) %all-reduce.6.cloned.1.call-update) | async-done | bytes 409616 | tf_op jit(solution)/shard_map/psum | solution.py:160
  630.3 8.4 %fusion.107 = f32[1600,960]{1,0:T(8,128)} fusion(bf16[256,1600]{1,0:T(8,128)(2,1)} %copy-done.3, f32[256,960]{0,1:T(8,128)} %copy-done.13, s32[256,960]{0,1:T(8,128)S(1)} %copy-done.6, f32[256,960]{0,1:T(8,128)S(1)} %get-tuple-element.18, f32[256]{0:T(256)S(1)} %get-tuple-element.13), kind=kOutput, calls=%fused_computation.126 | convolution fusion | flops 4723261440 | bytes 9913344 | tf_op jit(solution)/shard_map/dot_general | solution.py:164
  638.7 28.1 %psum.37 = f32[256]{0:T(256)S(1)} all-reduce(f32[256]{0:T(256)S(1)} %neg.22), channel_id=1, replica_groups=mesh['grp'=8,'gene'=16] {'gene'}, use_global_device_ids=true, to_apply=%region_16.17 | all-reduce | flops 256 | bytes 2048 | tf_op jit(solution)/shard_map/psum | solution.py:157
  667.4 52.5 %all-reduce.8.cloned.1.call-done = f32[1600,64]{0,1:T(8,128)} async-done(((f32[1600,64]{0,1:T(8,128)}), f32[1600,64]{0,1:T(8,128)}) %all-reduce.8.cloned.1.call-update) | async-done | bytes 409616 | tf_op jit(solution)/shard_map/psum | solution.py:160
  719.9 102.9 %reduce-scatter.8.cloned.1.call-done = f32[200,960]{1,0:T(8,128)} async-done(((f32[1600,960]{1,0:T(8,128)}), f32[200,960]{1,0:T(8,128)}) %reduce-scatter.8.cloned.1.call-update) | async-done | bytes 768016 | tf_op jit(solution)/shard_map/reduce_scatter | solution.py:163
  822.8 1.8 copy.169
  (63 shorter events, 6.9 us)
Async XLA Ops:
  7.2 470.8 %copy-start = (bf16[1600,960]{0,1:T(8,128)(2,1)S(1)}, bf16[1600,960]{0,1:T(8,128)(2,1)}, u32[]{:S(2)}) copy-start(bf16[1600,960]{0,1:T(8,128)(2,1)} %param.18) | copy-start | bytes 9216004
  7.2 196.1 %all-reduce.4.cloned.1.call-start = ((), (), s32[]{:S(2)}) async-start(), calls=%async_computation.3 | async-start | bytes 13107200 | tf_op jit(solution)/shard_map/psum | solution.py:107
  66.7 7.5 copy-start.8
  66.8 241.7 %reduce-scatter.10.cloned.1.call-start = ((), (), s32[]{:S(2)}) async-start(), calls=%async_computation.8 | async-start | bytes 7241728
  203.3 4.7 copy-start.2
  235.7 114.8 %all-gather.2.cloned.1.call-start = ((), (), s32[]{:S(2)}) async-start(), calls=%async_computation.4 | async-start | bytes 3620864 | tf_op jit(solution)/shard_map/all_gather | solution.py:125
  312.4 0.9 copy-start.4
  315.9 7.6 copy-start.9
  316.0 132.7 %reduce-scatter.12.cloned.1.call-start = ((), (), s32[]{:S(2)}) async-start(), calls=%async_computation.9 | async-start | bytes 7241728
  318.5 7.6 copy-start.11
  365.8 2.5 copy-start.7
  376.3 253.9 %all-reduce.6.cloned.1.call-start = ((), (), s32[]{:S(2)}) async-start(), calls=%async_computation.6 | async-start | bytes 851968 | tf_op jit(solution)/shard_map/psum | solution.py:160
  458.8 20.3 %copy-start.10 = (bf16[1600,64]{0,1:T(8,128)(2,1)S(1)}, bf16[1600,64]{0,1:T(8,128)(2,1)}, u32[]{:S(2)}) copy-start(bf16[1600,64]{0,1:T(8,128)(2,1)} %param.19) | copy-start | bytes 614404
  478.0 36.1 %copy-start.3 = (bf16[256,1600]{1,0:T(8,128)(2,1)}, bf16[256,1600]{1,0:T(8,128)(2,1)S(1)}, u32[]{:S(2)}) copy-start(bf16[256,1600]{1,0:T(8,128)(2,1)S(1)} %all_gather.7) | copy-start | bytes 2457604
  478.0 1.5 copy-start.5
  478.0 1.5 copy-start.12
  479.1 19.4 %copy-start.13 = (f32[256,960]{0,1:T(8,128)}, f32[256,960]{0,1:T(8,128)S(1)}, u32[]{:S(2)}) copy-start(f32[256,960]{0,1:T(8,128)S(1)} %fusion.249) | copy-start | bytes 2949124
  498.6 131.7 %copy-start.6 = (s32[256,960]{0,1:T(8,128)S(1)}, s32[256,960]{0,1:T(8,128)}, u32[]{:S(2)}) copy-start(s32[256,960]{0,1:T(8,128)} %param.10) | copy-start | bytes 2949124
  515.4 204.5 %all-reduce.8.cloned.1.call-start = ((), (), s32[]{:S(2)}) async-start(), calls=%async_computation.7 | async-start | bytes 851968 | tf_op jit(solution)/shard_map/psum | solution.py:160
  630.2 192.6 %reduce-scatter.8.cloned.1.call-start = ((), (), s32[]{:S(2)}) async-start(), calls=%async_computation.5 | async-start | bytes 7372800 | tf_op jit(solution)/shard_map/reduce_scatter | solution.py:163
  638.7 185.9 %copy-start.1 = (bf16[1600,960]{0,1:T(8,128)(2,1)S(1)}, bf16[1600,960]{0,1:T(8,128)(2,1)}, u32[]{:S(2)}) copy-start(bf16[1600,960]{0,1:T(8,128)(2,1)} %param.18) | copy-start | bytes 9216004
Sparse Core Ops, SparseCore 0:
  66.9 136.3 all-reduce.3
  235.9 72.5 reduce-scatter.9
  316.1 34.4 all-gather.1
  376.5 72.1 reduce-scatter.11
  515.5 114.6 all-reduce.5
  632.5 87.3 all-reduce.7
  724.4 98.4 reduce-scatter.7
